TPU v7x, 32 devices: a whole 2x2x4 slice. The times are simulated.
32 devices in a mesh: groups: 2 (over x), row: 8 (over z, y), col: 2 (over core).
Axes of the slice: x: 2, y: 2, z: 4, core: 2. Of those that a mesh axis runs over, the one named last changes fastest.
Arguments:
- start_field: float32 [1024, 384, 256], P(('groups', 'row'), 'col'), parts along dimension 0, may hold values from 0 to 2
- counts: int32 [1024, 384, 256], P('groups', 'row', 'col'), parts along dimension 0, may hold values from -40 to 40
- weights: int32 [1024, 384, 256], P('groups', 'row', 'col'), parts along dimension 0, may hold values from 1 to 16
- strat_one: int32 [512, 512], replicated, may hold values from -64 to 63
- strat_two: int32 [384, 384], replicated, may hold values from -64 to 63
- strat_three: int32 [256, 256], replicated, may hold values from -64 to 63
Outputs:
- estimate: float32 [1024, 384, 256], P(('groups', 'row'), 'col'), parts along dimension 0
There are 2 independent parts, one for each index of `groups`. A program takes and returns all parts, laid end to end along the dimension named above; an argument that names none is the same for every part. Nothing has to cross between parts.
All inputs are finite; a program needn't handle non-finite values.
Results may differ from a plain program's by a relative error of at most 0.0001.
Values sent between devices are 32-bit elements; how exact they have to be, the bound alone decides.
No kernel may reach another device: no remote copies, remote signals or barrier semaphores. Data moves between devices by JAX's collectives and lax.ppermute only.
A program may use at most 128 MiB of HBM per device.

v0:
```python
import math
import jax
import jax.numpy as jnp
from jax import lax
from jax.sharding import PartitionSpec as P

highest = lax.Precision.HIGHEST
step_size = 0.5


def scaled(quant):
    order = quant.shape[0]
    return quant.astype(jnp.float32) * (1.0 / (37.0 * math.sqrt(order)))


def along_first(matrix, field):
    return jnp.einsum("ji,iab->jab", matrix, field, precision=highest)


def along_second(matrix, field):
    return jnp.einsum("ji,aib->ajb", matrix, field, precision=highest)


def along_third(matrix, field):
    return jnp.einsum("ji,abi->abj", matrix, field, precision=highest)


def pencil_forward(field, first, second, third):
    field = along_third(third, field)
    field = along_second(
        second, lax.all_to_all(field, "col", split_axis=2, concat_axis=1, tiled=True)
    )
    return along_first(first, lax.all_to_all(field, "row", split_axis=1, concat_axis=0, tiled=True))


def pencil_adjoint(field, first, second, third):
    field = along_first(first.T, field)
    field = along_second(
        second.T, lax.all_to_all(field, "row", split_axis=0, concat_axis=1, tiled=True)
    )
    return along_third(
        third.T, lax.all_to_all(field, "col", split_axis=1, concat_axis=2, tiled=True)
    )


def per_device(start_field, counts, weights, strat_one, strat_two, strat_three):
    first = scaled(strat_one)
    second = scaled(strat_two)
    third = scaled(strat_three)
    weight_field = weights.astype(jnp.float32) / 16.0
    target = counts.astype(jnp.float32) / 16.0
    estimate = start_field
    image = pencil_forward(estimate, first, second, third)
    residual = weight_field * (image - target)
    gradient = pencil_adjoint(residual, first, second, third)
    estimate = jnp.maximum(estimate - step_size * gradient, 0.0)
    return estimate


def solution(mesh):
    placed = (
        P(("groups", "row"), "col", None),
        P("groups", "row", "col"),
        P("groups", "row", "col"),
        P(),
        P(),
        P(),
    )
    return jax.shard_map(
        per_device,
        mesh=mesh,
        in_specs=placed,
        out_specs=P(("groups", "row"), "col", None),
        check_vma=False,
    )
```

profile of v0, /device:TPU:0, one launch (start us, length us, event | category | flops | bytes accessed | tf_op | source)
XLA Modules:
  0.0 937.4 jit_solution(8232785942097816457)
XLA Ops:
  0.0 14.9 %convolution_bitcast_fusion.2 = f32[64,192,256]{2,1,0:T(8,128)} fusion(f32[64,192,256]{2,1,0:T(8,128)} %param.6, s32[256,256]{1,0:T(8,128)} %param.11), kind=kOutput, calls=%fused_computation.13 | convolution fusion | flops 9663807488 | bytes 25427968 | tf_op jit(solution)/shard_map/ji,abi->abj/dot_general | solution.py:25
  14.9 17.4 %copy.37 = f32[64,192,256]{1,0,2:T(8,128)} copy(f32[64,192,256]{2,1,0:T(8,128)} %convolution_bitcast_fusion.2) | data formatting | bytes 25165824 | tf_op jit(solution)/shard_map/ji,abi->abj/dot_general | solution.py:25
  32.3 31.8 %all_to_all.72 = f32[64,192,256]{1,0,2:T(8,128)} all-to-all(f32[64,192,256]{1,0,2:T(8,128)} %copy.37), channel_id=1, replica_groups=mesh['groups'=2,'row'=8,'col'=2] {'col'}, dimensions={2} | all-to-all | bytes 25165824 | tf_op jit(solution)/shard_map/all_to_all | solution.py:31
  64.1 17.9 %copy.57 = f32[64,192,2,128]{3,2,1,0:T(2,128)} copy(f32[64,192,2,128]{1,0,3,2:T(8,128)} %bitcast.42) | data formatting | bytes 25165824 | tf_op jit(solution)/shard_map/all_to_all | solution.py:31
  82.1 0.0 copy-start.1
  82.1 11.0 %copy.39 = f32[64,2,192,128]{3,2,1,0:T(8,128)} copy(f32[64,2,192,128]{3,1,2,0:T(2,128)} %bitcast.44) | data formatting | bytes 25165824 | tf_op jit(solution)/shard_map/all_to_all | solution.py:31
  93.0 0.0 copy-done.1
  93.0 43.6 %convolution_bitcast_fusion.1 = f32[64,384,128]{1,2,0:T(8,128)} fusion(f32[64,384,128]{2,1,0:T(8,128)} %bitcast.40, s32[384,384]{1,0:T(8,128)S(1)} %copy-done.1), kind=kOutput, calls=%fused_computation.12 | convolution fusion | flops 14495809536 | bytes 25755648 | tf_op jit(solution)/shard_map/ji,aib->ajb/dot_general | solution.py:21
  136.6 12.7 %copy.41 = f32[64,384,128]{2,0,1:T(8,128)} copy(f32[64,384,128]{1,2,0:T(8,128)} %convolution_bitcast_fusion.1) | data formatting | bytes 25165824 | tf_op jit(solution)/shard_map/ji,aib->ajb/transpose | solution.py:21
  149.4 281.8 %all_to_all.73 = f32[64,384,128]{2,0,1:T(8,128)} all-to-all(f32[64,384,128]{2,0,1:T(8,128)} %copy.41), channel_id=1, replica_groups=mesh['groups'=2,'row'=8,'col'=2] {'row'}, dimensions={1} | all-to-all | bytes 25165824 | tf_op jit(solution)/shard_map/all_to_all | solution.py:33
  431.2 0.0 copy-start
  431.2 16.5 %copy.43 = f32[8,64,48,128]{3,2,1,0:T(8,128)} copy(f32[8,64,48,128]{3,1,2,0:T(8,128)} %bitcast.45) | data formatting | bytes 25165824 | tf_op jit(solution)/shard_map/all_to_all | solution.py:33
  447.7 0.0 copy-done
  447.7 28.6 %fusion.5 = f32[512,48,128]{2,0,1:T(8,128)S(1)} fusion(f32[512,48,128]{2,1,0:T(8,128)} %bitcast.43, s32[512,512]{1,0:T(8,128)S(1)} %copy-done), kind=kOutput, calls=%fused_computation.5 | convolution fusion | flops 19327877120 | bytes 26214400 | tf_op jit(solution)/shard_map/ji,iab->jab/dot_general | solution.py:17
  476.4 38.4 %fusion.3 = f32[512,48,128]{2,0,1:T(8,128)} fusion(f32[512,48,128]{2,0,1:T(8,128)S(1)} %fusion.5, s32[512,48,128]{2,1,0:T(8,128)} %param.7, s32[512,48,128]{2,1,0:T(8,128)} %param.8, s32[512,512]{1,0:T(8,128)S(1)} %copy-done), kind=kOutput, calls=%fused_computation.4 | convolution fusion | flops 19346751488 | bytes 51380224 | tf_op jit(solution)/shard_map/ji,iab->jab/dot_general | solution.py:17
  514.8 16.4 %copy.47 = f32[512,48,128]{2,1,0:T(8,128)} copy(f32[512,48,128]{2,0,1:T(8,128)} %fusion.3) | data formatting | bytes 25165824 | tf_op jit(solution)/shard_map/ji,iab->jab/dot_general | solution.py:17
  531.2 279.9 %all_to_all.74 = f32[512,48,128]{2,1,0:T(8,128)} all-to-all(f32[512,48,128]{2,1,0:T(8,128)} %copy.47), channel_id=1, replica_groups=mesh['groups'=2,'row'=8,'col'=2] {'row'}, dimensions={0} | all-to-all | bytes 25165824 | tf_op jit(solution)/shard_map/all_to_all | solution.py:39
  811.1 11.2 %copy.48 = f32[64,8,48,128]{3,2,1,0:T(8,128)} copy(f32[64,8,48,128]{3,2,0,1:T(8,128)} %bitcast.46) | data formatting | bytes 25165824 | tf_op jit(solution)/shard_map/all_to_all | solution.py:39
  822.3 27.5 %convolution_bitcast_fusion = f32[64,384,128]{1,2,0:T(8,128)} fusion(f32[64,384,128]{2,1,0:T(8,128)} %bitcast.41, s32[384,384]{1,0:T(8,128)S(1)} %copy-done.1), kind=kOutput, calls=%fused_computation.11 | convolution fusion | flops 14495809536 | bytes 25755648 | tf_op jit(solution)/shard_map/ji,aib->ajb/dot_general | solution.py:21
  849.8 12.6 %copy.50 = f32[64,384,128]{2,0,1:T(8,128)} copy(f32[64,384,128]{1,2,0:T(8,128)} %convolution_bitcast_fusion) | data formatting | bytes 25165824 | tf_op jit(solution)/shard_map/ji,aib->ajb/transpose | solution.py:21
  862.4 15.9 %all_to_all.75 = f32[64,384,128]{2,0,1:T(8,128)S(1)} all-to-all(f32[64,384,128]{2,0,1:T(8,128)} %copy.50), channel_id=1, replica_groups=mesh['groups'=2,'row'=8,'col'=2] {'col'}, dimensions={1} | all-to-all | bytes 25165824 | tf_op jit(solution)/shard_map/all_to_all | solution.py:42
  878.3 23.4 %copy.52 = f32[64,192,2,128]{3,2,1,0:T(2,128)} copy(f32[64,192,2,128]{3,0,1,2:T(8,128)S(1)} %bitcast.47) | data formatting | bytes 25165824 | tf_op jit(solution)/shard_map/all_to_all | solution.py:42
  901.7 0.0 copy-start.2
  901.7 16.6 %all_to_all.67 = f32[64,192,256]{2,1,0:T(8,128)} reshape(f32[64,192,2,128]{3,2,1,0:T(2,128)} %copy.52) | data formatting | bytes 25165824 | tf_op jit(solution)/shard_map/all_to_all | solution.py:42
  918.3 0.0 copy-done.2
  918.3 18.6 %subtract_maximum_fusion = f32[64,192,256]{2,1,0:T(8,128)} fusion(f32[64,192,256]{2,1,0:T(8,128)} %param.6, f32[64,192,256]{2,1,0:T(8,128)} %all_to_all.67, s32[256,256]{1,0:T(8,128)S(1)} %copy-done.2), kind=kOutput, calls=%fused_computation.9 | convolution fusion | flops 9673244672 | bytes 38010880 | tf_op jit(solution)/shard_map/ji,abi->abj/dot_general | solution.py:25
Async XLA Ops:
  82.1 11.0 %copy-start.1 = (s32[384,384]{1,0:T(8,128)S(1)}, s32[384,384]{1,0:T(8,128)}, u32[]{:S(2)}) copy-start(s32[384,384]{1,0:T(8,128)} %param.10) | copy-start | bytes 1769476
  431.2 16.5 %copy-start = (s32[512,512]{1,0:T(8,128)S(1)}, s32[512,512]{1,0:T(8,128)}, u32[]{:S(2)}) copy-start(s32[512,512]{1,0:T(8,128)} %param.9) | copy-start | bytes 3145732
  901.7 16.6 %copy-start.2 = (s32[256,256]{1,0:T(8,128)S(1)}, s32[256,256]{1,0:T(8,128)}, u32[]{:S(2)}) copy-start(s32[256,256]{1,0:T(8,128)} %param.11) | copy-start | bytes 786436
where the time goes:
time: 943 us; the launch traced here: 937 us
  blocking collectives  609 us (65%)
  matrix products  172 us (18%)
  local copies, waits for them, and re-layouts  156 us (17%)
    all_to_all x1, blocking collectives, pencil_forward(): lax.all_to_all(field, 'row', split_axis=1, concat_axis=0, tiled=True)  282 us
    all_to_all x1, blocking collectives, pencil_adjoint(): lax.all_to_all(field, 'row', split_axis=0, concat_axis=1, tiled=True)  280 us
    dot_general x2, matrix products, along_second(): return jnp.einsum('ji,aib->ajb', matrix, field, precision=highest)  71.1 us
    dot_general x2, matrix products, along_first(): return jnp.einsum('ji,iab->jab', matrix, field, precision=highest)  67 us
    all_to_all x2, local copies, waits for them, and re-layouts, pencil_adjoint(): lax.all_to_all(field, 'col', split_axis=1, concat_axis=2, tiled=True)  39.9 us
    dot_general x2, matrix products, along_third(): return jnp.einsum('ji,abi->abj', matrix, field, precision=highest)  33.5 us
    all_to_all x1, blocking collectives, pencil_forward(): lax.all_to_all(field, 'col', split_axis=2, concat_axis=1, tiled=True)  31.8 us
    all_to_all x2, local copies, waits for them, and re-layouts, pencil_forward(): lax.all_to_all(field, 'col', split_axis=2, concat_axis=1, tiled=True)  28.9 us

commit v1 on v0

--- a/solution.py
+++ b/solution.py
@@ -6,6 +6,13 @@
 
 highest = lax.Precision.HIGHEST
 step_size = 0.5
+
+
+def trade_parts(x, axis, split, join):
+    count = lax.axis_size(axis)
+    blocks = jnp.stack(jnp.split(x, count, axis=split), axis=0)
+    blocks = lax.all_to_all(blocks, axis, split_axis=0, concat_axis=0)
+    return jnp.concatenate(blocks, axis=join)
 
 
 def scaled(quant):
@@ -30,7 +37,7 @@
     field = along_second(
         second, lax.all_to_all(field, "col", split_axis=2, concat_axis=1, tiled=True)
     )
-    return along_first(first, lax.all_to_all(field, "row", split_axis=1, concat_axis=0, tiled=True))
+    return along_first(first, trade_parts(field, "row", 1, 0))
 
 
 def pencil_adjoint(field, first, second, third):

time: 943 us -> 984 us (1.043)
  local copies, waits for them, and re-layouts: 156 us -> 203 us
    another operation x0 -> x10, local copies, waits for them, and re-layouts: none -> 56.1 us  [trade_parts(): blocks = jnp.stack(jnp.split(x, count, axis=split), axis=0)]
    transpose x2 -> x1, local copies, waits for them, and re-layouts: 25.4 us -> 12.6 us  [along_second(): return jnp.einsum('ji,aib->ajb', matrix, field, precision=highest)]
where the time goes in v1:
time: 984 us; the launch traced here: 978 us
  blocking collectives  608 us (62%)
  local copies, waits for them, and re-layouts  203 us (21%)
  matrix products  167 us (17%)
    all_to_all x1, blocking collectives, trade_parts(): blocks = lax.all_to_all(blocks, axis, split_axis=0, concat_axis=0)  281 us
    all_to_all x1, blocking collectives, pencil_adjoint(): lax.all_to_all(field, 'row', split_axis=0, concat_axis=1, tiled=True)  280 us
    dot_general x2, matrix products, along_second(): return jnp.einsum('ji,aib->ajb', matrix, field, precision=highest)  71.1 us
    dot_general x2, matrix products, along_first(): return jnp.einsum('ji,iab->jab', matrix, field, precision=highest)  62 us
    another operation x10, local copies, waits for them, and re-layouts, trade_parts(): blocks = jnp.stack(jnp.split(x, count, axis=split), axis=0)  56.1 us
    all_to_all x2, local copies, waits for them, and re-layouts, pencil_adjoint(): lax.all_to_all(field, 'col', split_axis=1, concat_axis=2, tiled=True)  40 us
    dot_general x2, matrix products, along_third(): return jnp.einsum('ji,abi->abj', matrix, field, precision=highest)  33.5 us
    all_to_all x1, blocking collectives, pencil_forward(): lax.all_to_all(field, 'col', split_axis=2, concat_axis=1, tiled=True)  31.8 us

profile of v1, /device:TPU:0, one launch (start us, length us, event | category | flops | bytes accessed | tf_op | source)
XLA Modules:
  0.0 978.2 jit_solution(9219939643596086590)
XLA Ops:
  0.0 14.9 %convolution_bitcast_fusion.2 = f32[64,192,256]{2,1,0:T(8,128)} fusion(f32[64,192,256]{2,1,0:T(8,128)} %param.6, s32[256,256]{1,0:T(8,128)} %param.11), kind=kOutput, calls=%fused_computation.11 | convolution fusion | flops 9663807488 | bytes 25427968 | tf_op jit(solution)/shard_map/ji,abi->abj/dot_general | solution.py:32
  14.9 17.4 %copy.40 = f32[64,192,256]{1,0,2:T(8,128)} copy(f32[64,192,256]{2,1,0:T(8,128)} %convolution_bitcast_fusion.2) | data formatting | bytes 25165824 | tf_op jit(solution)/shard_map/ji,abi->abj/dot_general | solution.py:32
  32.3 31.8 %all_to_all.59 = f32[64,192,256]{1,0,2:T(8,128)} all-to-all(f32[64,192,256]{1,0,2:T(8,128)} %copy.40), channel_id=1, replica_groups=mesh['groups'=2,'row'=8,'col'=2] {'col'}, dimensions={2} | all-to-all | bytes 25165824 | tf_op jit(solution)/shard_map/all_to_all | solution.py:38
  64.2 17.9 %copy.65 = f32[64,192,2,128]{3,2,1,0:T(2,128)} copy(f32[64,192,2,128]{1,0,3,2:T(8,128)} %bitcast.56) | data formatting | bytes 25165824 | tf_op jit(solution)/shard_map/all_to_all | solution.py:38
  82.1 0.0 copy-start.3
  82.1 10.9 %copy.42 = f32[64,2,192,128]{3,2,1,0:T(8,128)} copy(f32[64,2,192,128]{3,1,2,0:T(2,128)} %bitcast.58) | data formatting | bytes 25165824 | tf_op jit(solution)/shard_map/all_to_all | solution.py:38
  93.0 0.0 copy-done.3
  93.0 43.6 %convolution_bitcast_fusion.1 = f32[64,384,128]{1,2,0:T(8,128)} fusion(f32[64,384,128]{2,1,0:T(8,128)} %bitcast.54, s32[384,384]{1,0:T(8,128)S(1)} %copy-done.3), kind=kOutput, calls=%fused_computation.10 | convolution fusion | flops 14495809536 | bytes 25755648 | tf_op jit(solution)/shard_map/ji,aib->ajb/dot_general | solution.py:28
  136.6 28.2 %slice_bitcast_fusion = (f32[1,64,48,128]{2,3,1,0:T(8,128)}, f32[1,64,48,128]{2,3,1,0:T(8,128)}, f32[1,64,48,128]{2,3,1,0:T(8,128)}, f32[1,64,48,128]{2,3,1,0:T(...) fusion(f32[64,384,128]{1,2,0:T(8,128)} %convolution_bitcast_fus, ...), kind=kLoop, calls=%fused_computation.12 | loop fusion | bytes 25165824 | tf_op jit(solution)/shard_map/stack | solution.py:13
  164.9 2.8 copy.51
  167.7 2.8 copy.50
  170.5 3.7 copy.49
  174.2 3.7 copy.48
  177.9 3.7 copy.47
  181.6 3.7 copy.46
  185.3 3.7 copy.45
  189.0 3.7 copy.44
  192.7 0.0 copy-start.1
  192.7 0.0 copy-start
  192.7 1.7 constant_dynamic-update-slice_fusion.7
  194.4 1.5 constant_dynamic-update-slice_fusion.6
  195.9 1.5 constant_dynamic-update-slice_fusion.5
  197.4 1.5 constant_dynamic-update-slice_fusion.4
  198.9 0.0 copy-done.1
  198.9 0.1 constant_dynamic-update-slice_fusion.3
  199.0 0.0 copy-done
  199.0 0.1 constant_dynamic-update-slice_fusion.2
  199.2 0.1 constant_dynamic-update-slice_fusion.1
  199.3 0.1 constant_dynamic-update-slice_fusion
  199.4 280.8 %all_to_all.60 = f32[8,64,48,128]{3,2,1,0:T(8,128)} all-to-all(f32[8,64,48,128]{3,2,1,0:T(8,128)S(1)} %constant_dynamic-update-slice_fusion), channel_id=1, replica_groups=mesh['groups'=2,'row'=8,'col'=2] {'row'}, dimensions={0} | all-to-all | bytes 25165824 | tf_op jit(solution)/shard_map/all_to_all | solution.py:14
  480.2 0.0 copy-start.2
  480.2 13.5 %copy.52 = f32[8,64,48,128]{3,1,0,2:T(8,128)} copy(f32[8,64,48,128]{3,2,1,0:T(8,128)} %all_to_all.60) | data formatting | bytes 25165824 | tf_op jit(solution)/shard_map/all_to_all | solution.py:14
  493.6 0.0 copy-done.2
  493.6 23.6 %fusion.8 = f32[512,48,128]{2,0,1:T(8,128)S(1)} fusion(f32[512,48,128]{2,0,1:T(8,128)} %bitcast.57, s32[512,512]{1,0:T(8,128)S(1)} %copy-done.2), kind=kOutput, calls=%fused_computation.20 | convolution fusion | flops 19327877120 | bytes 26214400 | tf_op jit(solution)/shard_map/ji,iab->jab/dot_general | solution.py:24
  517.2 38.5 %fusion.3 = f32[512,48,128]{2,0,1:T(8,128)} fusion(f32[512,48,128]{2,0,1:T(8,128)S(1)} %fusion.8, s32[512,48,128]{2,1,0:T(8,128)} %param.7, s32[512,48,128]{2,1,0:T(8,128)} %param.8, s32[512,512]{1,0:T(8,128)S(1)} %copy-done.2), kind=kOutput, calls=%fused_computation.4 | convolution fusion | flops 19346751488 | bytes 51380224 | tf_op jit(solution)/shard_map/ji,iab->jab/dot_general | solution.py:24
  555.7 16.4 %copy.55 = f32[512,48,128]{2,1,0:T(8,128)} copy(f32[512,48,128]{2,0,1:T(8,128)} %fusion.3) | data formatting | bytes 25165824 | tf_op jit(solution)/shard_map/ji,iab->jab/dot_general | solution.py:24
  572.1 279.7 %all_to_all.61 = f32[512,48,128]{2,1,0:T(8,128)} all-to-all(f32[512,48,128]{2,1,0:T(8,128)} %copy.55), channel_id=1, replica_groups=mesh['groups'=2,'row'=8,'col'=2] {'row'}, dimensions={0} | all-to-all | bytes 25165824 | tf_op jit(solution)/shard_map/all_to_all | solution.py:46
  851.8 0.0 copy-start.4
  851.8 11.3 %copy.56 = f32[64,8,48,128]{3,2,1,0:T(8,128)} copy(f32[64,8,48,128]{3,2,0,1:T(8,128)} %bitcast.59) | data formatting | bytes 25165824 | tf_op jit(solution)/shard_map/all_to_all | solution.py:46
  863.0 0.0 copy-done.4
  863.0 27.5 %convolution_bitcast_fusion = f32[64,384,128]{1,2,0:T(8,128)} fusion(f32[64,384,128]{2,1,0:T(8,128)} %bitcast.55, s32[384,384]{1,0:T(8,128)S(1)} %copy-done.4), kind=kOutput, calls=%fused_computation.9 | convolution fusion | flops 14495809536 | bytes 25755648 | tf_op jit(solution)/shard_map/ji,aib->ajb/dot_general | solution.py:28
  890.5 12.6 %copy.58 = f32[64,384,128]{2,0,1:T(8,128)} copy(f32[64,384,128]{1,2,0:T(8,128)} %convolution_bitcast_fusion) | data formatting | bytes 25165824 | tf_op jit(solution)/shard_map/ji,aib->ajb/transpose | solution.py:28
  903.1 15.9 %all_to_all.62 = f32[64,384,128]{2,0,1:T(8,128)S(1)} all-to-all(f32[64,384,128]{2,0,1:T(8,128)} %copy.58), channel_id=1, replica_groups=mesh['groups'=2,'row'=8,'col'=2] {'col'}, dimensions={1} | all-to-all | bytes 25165824 | tf_op jit(solution)/shard_map/all_to_all | solution.py:49
  919.1 23.4 %copy.60 = f32[64,192,2,128]{3,2,1,0:T(2,128)} copy(f32[64,192,2,128]{3,0,1,2:T(8,128)S(1)} %bitcast.60) | data formatting | bytes 25165824 | tf_op jit(solution)/shard_map/all_to_all | solution.py:49
  942.4 0.0 copy-start.5
  942.4 16.6 %all_to_all.54 = f32[64,192,256]{2,1,0:T(8,128)} reshape(f32[64,192,2,128]{3,2,1,0:T(2,128)} %copy.60) | data formatting | bytes 25165824 | tf_op jit(solution)/shard_map/all_to_all | solution.py:49
  959.0 0.0 copy-done.5
  959.0 18.6 %subtract_maximum_fusion = f32[64,192,256]{2,1,0:T(8,128)} fusion(f32[64,192,256]{2,1,0:T(8,128)} %param.6, f32[64,192,256]{2,1,0:T(8,128)} %all_to_all.54, s32[256,256]{1,0:T(8,128)S(1)} %copy-done.5), kind=kOutput, calls=%fused_computation.7 | convolution fusion | flops 9673244672 | bytes 38010880 | tf_op jit(solution)/shard_map/ji,abi->abj/dot_general | solution.py:32
Async XLA Ops:
  82.1 10.9 %copy-start.3 = (s32[384,384]{1,0:T(8,128)S(1)}, s32[384,384]{1,0:T(8,128)}, u32[]{:S(2)}) copy-start(s32[384,384]{1,0:T(8,128)} %param.10) | copy-start | bytes 1769476
  192.7 6.2 copy-start.1
  192.7 6.3 copy-start
  480.2 13.5 %copy-start.2 = (s32[512,512]{1,0:T(8,128)S(1)}, s32[512,512]{1,0:T(8,128)}, u32[]{:S(2)}) copy-start(s32[512,512]{1,0:T(8,128)} %param.9) | copy-start | bytes 3145732
  851.8 11.3 %copy-start.4 = (s32[384,384]{1,0:T(8,128)S(1)}, s32[384,384]{1,0:T(8,128)}, u32[]{:S(2)}) copy-start(s32[384,384]{1,0:T(8,128)} %param.10) | copy-start | bytes 1769476
  942.4 16.6 %copy-start.5 = (s32[256,256]{1,0:T(8,128)S(1)}, s32[256,256]{1,0:T(8,128)}, u32[]{:S(2)}) copy-start(s32[256,256]{1,0:T(8,128)} %param.11) | copy-start | bytes 786436
